TPU v7x, 128 devices: a whole 4x4x4 slice. The times are simulated.
128 devices in a mesh: ctx: 64 (over z, x, y), wsh: 2 (over core).
Axes of the slice: x: 4, y: 4, z: 4, core: 2. Of those that a mesh axis runs over, the one named last changes fastest.
Arguments:
- block_input: bfloat16 [2, 8192, 640], P('wsh', 'ctx'), may hold values from -6 to 6
- cotangent: float32 [2, 8192, 640], P('wsh', 'ctx'), may hold values from -6 to 6
- pair_blocks: int32 [64, 2], replicated, may hold values from 0 to 127, as said below
- w_query: bfloat16 [640, 1024], P(None, 'wsh'), may hold values from -0.25 to 0.25
- w_key: bfloat16 [640, 256], P(None, 'wsh'), may hold values from -0.25 to 0.25
- w_value: bfloat16 [640, 256], P(None, 'wsh'), may hold values from -0.25 to 0.25
- w_out: bfloat16 [1024, 640], P('wsh'), may hold values from -0.1875 to 0.1875
- w_gate: bfloat16 [640, 2048], P(None, 'wsh'), may hold values from -0.25 to 0.25
- w_up: bfloat16 [640, 2048], P(None, 'wsh'), may hold values from -0.25 to 0.25
- w_down: bfloat16 [2048, 640], P('wsh'), may hold values from -0.125 to 0.125
- attn_pre_gain: bfloat16 [640], P('wsh'), may hold values from -0.3984375 to 0.59765625
- query_gain: bfloat16 [256], P('wsh'), may hold values from -0.3984375 to 0.59765625
- key_gain: bfloat16 [256], P('wsh'), may hold values from -0.3984375 to 0.59765625
- attn_post_gain: bfloat16 [640], P('wsh'), may hold values from -0.3984375 to 0.59765625
- ffw_pre_gain: bfloat16 [640], P('wsh'), may hold values from -0.3984375 to 0.59765625
- ffw_post_gain: bfloat16 [640], P('wsh'), may hold values from -0.3984375 to 0.59765625
Outputs:
- block_output: float32 [2, 8192, 640], P('wsh', 'ctx')
- input_grad: float32 [2, 8192, 640], P('wsh', 'ctx')
- w_query_grad: float32 [640, 1024], P(None, 'wsh')
- w_key_grad: float32 [640, 256], P(None, 'wsh')
- w_value_grad: float32 [640, 256], P(None, 'wsh')
- w_out_grad: float32 [1024, 640], P('wsh')
- w_gate_grad: float32 [640, 2048], P(None, 'wsh')
- w_up_grad: float32 [640, 2048], P(None, 'wsh')
- w_down_grad: float32 [2048, 640], P('wsh')
- attn_pre_gain_grad: float32 [640], P('wsh')
- query_gain_grad: float32 [256], P('wsh')
- key_gain_grad: float32 [256], P('wsh')
- attn_post_gain_grad: float32 [640], P('wsh')
- ffw_pre_gain_grad: float32 [640], P('wsh')
- ffw_post_gain_grad: float32 [640], P('wsh')
Inputs may be any that keep to these rules, and one draw needn't show every extreme that they name: `pair_blocks`: row r holds a block b and its mirror 2 * 64 - 1 - b, in the order in which index r of ctx stores them; over all rows every one of the 128 blocks appears exactly once.
All inputs are finite; a program needn't handle non-finite values.
Results may differ from a plain program's by a relative error of at most 0.018.
Values may be sent and summed in bfloat16 or wider, within the bound.
No kernel may reach another device: no remote copies, remote signals or barrier semaphores. Data moves between devices by JAX's collectives and lax.ppermute only.
A program may use at most 192 MiB of HBM per device.

v0:
```python
import jax
import jax.numpy as jnp
from jax import lax
from jax.sharding import PartitionSpec as P

HEADS = 4
HDIM = 256
epsilon = 1e-06
theta_base = 1000000.0


def rms_forward(values, gain_w):
    factor = lax.rsqrt(jnp.mean(values * values, axis=-1, keepdims=True) + epsilon)
    return (values * factor * (1.0 + gain_w), factor)


def rms_backward(values, factor, gain_w, grad_out):
    weighted = grad_out * (1.0 + gain_w)
    inner = jnp.mean(weighted * values, axis=-1, keepdims=True)
    grad_in = factor * (weighted - values * factor * factor * inner)
    grad_gain = jnp.sum((grad_out * values * factor).reshape(-1, values.shape[-1]), axis=0)
    return (grad_in, grad_gain)


def rotary_tables(positions, width):
    half_width = width // 2
    frequency = theta_base ** (-jnp.arange(half_width, dtype=jnp.float32) * 2.0 / width)
    angles = positions.astype(jnp.float32)[:, None] * frequency[None, :]
    return (jnp.cos(angles)[:, None, :], jnp.sin(angles)[:, None, :])


def rotate(values, cos_tab, sin_tab):
    half_width = values.shape[-1] // 2
    first_half = values[..., :half_width]
    second_half = values[..., half_width:]
    return jnp.concatenate(
        [
            first_half * cos_tab - second_half * sin_tab,
            second_half * cos_tab + first_half * sin_tab,
        ],
        axis=-1,
    )


def rotate_back(grads, cos_tab, sin_tab):
    half_width = grads.shape[-1] // 2
    first_half = grads[..., :half_width]
    second_half = grads[..., half_width:]
    return jnp.concatenate(
        [
            first_half * cos_tab + second_half * sin_tab,
            second_half * cos_tab - first_half * sin_tab,
        ],
        axis=-1,
    )


def block_positions(block_ids, half_rows):
    offsets = jnp.arange(half_rows, dtype=jnp.int32)
    return (block_ids[:, None] * half_rows + offsets[None, :]).reshape(-1)


def dot_f32(left, right):
    return jnp.dot(left, right, preferred_element_type=jnp.float32)


def masked_scores(query_rot, key_all, query_pos, key_pos):
    scores = jnp.einsum(
        "qhd,kd->hqk", query_rot, key_all, preferred_element_type=jnp.float32
    ) * HDIM ** (-0.5)
    return jnp.where(key_pos[None, None, :] <= query_pos[None, :, None], scores, -1e30)


def per_device(
    block_input,
    cotangent,
    pair_blocks,
    w_query,
    w_key,
    w_value,
    w_out,
    w_gate,
    w_up,
    w_down,
    attn_pre_gain,
    query_gain,
    key_gain,
    attn_post_gain,
    ffw_pre_gain,
    ffw_post_gain,
):
    row_count = block_input.shape[1]
    half_rows = row_count // 2
    my_rank = lax.axis_index("ctx")
    resid_in = block_input[0].astype(jnp.float32)
    grad_top = cotangent[0]
    my_blocks = lax.dynamic_slice_in_dim(pair_blocks, my_rank, 1, 0)[0]
    query_pos = block_positions(my_blocks, half_rows)
    key_pos = block_positions(pair_blocks.reshape(-1), half_rows)
    cos_tab, sin_tab = rotary_tables(query_pos, HDIM)
    (
        query_w,
        key_w,
        value_w,
        out_w,
        gate_w,
        up_w,
        down_w,
        gain_one,
        gain_query,
        gain_key,
        gain_two,
        gain_three,
        gain_four,
    ) = (
        lax.all_gather(w_query, "wsh", axis=1, tiled=True),
        lax.all_gather(w_key, "wsh", axis=1, tiled=True),
        lax.all_gather(w_value, "wsh", axis=1, tiled=True),
        lax.all_gather(w_out, "wsh", axis=0, tiled=True),
        lax.all_gather(w_gate, "wsh", axis=1, tiled=True),
        lax.all_gather(w_up, "wsh", axis=1, tiled=True),
        lax.all_gather(w_down, "wsh", axis=0, tiled=True),
        lax.all_gather(attn_pre_gain, "wsh", axis=0, tiled=True),
        lax.all_gather(query_gain, "wsh", axis=0, tiled=True),
        lax.all_gather(key_gain, "wsh", axis=0, tiled=True),
        lax.all_gather(attn_post_gain, "wsh", axis=0, tiled=True),
        lax.all_gather(ffw_pre_gain, "wsh", axis=0, tiled=True),
        lax.all_gather(ffw_post_gain, "wsh", axis=0, tiled=True),
    )
    gain_one = gain_one.astype(jnp.float32)
    gain_query = gain_query.astype(jnp.float32)
    gain_key = gain_key.astype(jnp.float32)
    gain_two = gain_two.astype(jnp.float32)
    normed_one, factor_one = rms_forward(resid_in, gain_one)
    attn_in = normed_one.astype(jnp.bfloat16)
    query_raw = dot_f32(attn_in, query_w).reshape(row_count, HEADS, HDIM)
    key_raw = dot_f32(attn_in, key_w)[:, None, :]
    value_bf = dot_f32(attn_in, value_w).astype(jnp.bfloat16)
    query_normed, query_factor = rms_forward(query_raw, gain_query)
    key_normed, key_factor = rms_forward(key_raw, gain_key)
    query_rot = rotate(query_normed, cos_tab, sin_tab).astype(jnp.bfloat16)
    key_rot = rotate(key_normed, cos_tab, sin_tab)[:, 0, :].astype(jnp.bfloat16)
    key_all, value_all = (
        lax.all_gather(key_rot, "ctx", axis=0, tiled=True),
        lax.all_gather(value_bf, "ctx", axis=0, tiled=True),
    )
    scores = masked_scores(query_rot, key_all, query_pos, key_pos)
    top_score = jnp.max(scores, axis=-1, keepdims=True)
    shifted = jnp.exp(scores - top_score)
    totals = jnp.sum(shifted, axis=-1, keepdims=True)
    probs = (shifted / totals).astype(jnp.bfloat16)
    log_total = top_score[..., 0] + jnp.log(totals[..., 0])
    attn_heads = jnp.einsum(
        "hqk,kd->qhd", probs, value_all, preferred_element_type=jnp.float32
    ).astype(jnp.bfloat16)
    attn_out = attn_heads.reshape(row_count, HEADS * HDIM)
    attn_proj = dot_f32(attn_out, out_w)
    normed_two, factor_two = rms_forward(attn_proj, gain_two)
    mid = resid_in + normed_two
    gain_three = gain_three.astype(jnp.float32)
    gain_four = gain_four.astype(jnp.float32)
    normed_three, factor_three = rms_forward(mid, gain_three)
    ffw_in = normed_three.astype(jnp.bfloat16)
    gate = dot_f32(ffw_in, gate_w)
    up_val = dot_f32(ffw_in, up_w)
    activated, gelu_back = jax.vjp(lambda inner: jax.nn.gelu(inner, approximate=True), gate)
    hidden = (activated * up_val).astype(jnp.bfloat16)
    ffw_proj = dot_f32(hidden, down_w)
    normed_four, factor_four = rms_forward(ffw_proj, gain_four)
    block_output = mid + normed_four
    grad_ffw, grad_gain_four = rms_backward(ffw_proj, factor_four, gain_four, grad_top)
    grad_ffw_bf = grad_ffw.astype(jnp.bfloat16)
    grad_w_down = dot_f32(hidden.T, grad_ffw_bf)
    grad_hidden = dot_f32(grad_ffw_bf, down_w.T)
    grad_gate = gelu_back(grad_hidden * up_val)[0].astype(jnp.bfloat16)
    grad_up = (grad_hidden * activated).astype(jnp.bfloat16)
    grad_w_gate = dot_f32(ffw_in.T, grad_gate)
    grad_w_up = dot_f32(ffw_in.T, grad_up)
    grad_ffw_in = dot_f32(grad_gate, gate_w.T) + dot_f32(grad_up, up_w.T)
    grad_mid_part, grad_gain_three = rms_backward(mid, factor_three, gain_three, grad_ffw_in)
    grad_mid = grad_top + grad_mid_part
    grad_proj, grad_gain_two = rms_backward(attn_proj, factor_two, gain_two, grad_mid)
    grad_proj_bf = grad_proj.astype(jnp.bfloat16)
    grad_w_out = dot_f32(attn_out.T, grad_proj_bf)
    grad_attn = dot_f32(grad_proj_bf, out_w.T).astype(jnp.bfloat16)
    grad_heads = grad_attn.reshape(row_count, HEADS, HDIM)
    delta = jnp.sum(grad_heads.astype(jnp.float32) * attn_heads.astype(jnp.float32), axis=-1).T
    scores_again = masked_scores(query_rot, key_all, query_pos, key_pos)
    probs_again = jnp.exp(scores_again - log_total[:, :, None])
    grad_probs = jnp.einsum(
        "qhd,kd->hqk", grad_heads, value_all, preferred_element_type=jnp.float32
    )
    grad_scores = (probs_again * (grad_probs - delta[:, :, None])).astype(jnp.bfloat16)
    grad_query = jnp.einsum(
        "hqk,kd->qhd", grad_scores, key_all, preferred_element_type=jnp.float32
    ) * HDIM ** (-0.5)
    grad_key_part = jnp.einsum(
        "hqk,qhd->kd", grad_scores, query_rot, preferred_element_type=jnp.float32
    ) * HDIM ** (-0.5)
    grad_value_part = jnp.einsum(
        "hqk,qhd->kd",
        probs_again.astype(jnp.bfloat16),
        grad_heads,
        preferred_element_type=jnp.float32,
    )
    kv_terms = jnp.concatenate([grad_key_part, grad_value_part], axis=1)
    kv_mine = lax.psum_scatter(kv_terms, "ctx", scatter_dimension=0, tiled=True)
    grad_key = kv_mine[:, :HDIM]
    grad_value = kv_mine[:, HDIM:]
    grad_query_raw, grad_gain_query = rms_backward(
        query_raw, query_factor, gain_query, rotate_back(grad_query, cos_tab, sin_tab)
    )
    grad_key_raw, grad_gain_key = rms_backward(
        key_raw, key_factor, gain_key, rotate_back(grad_key[:, None, :], cos_tab, sin_tab)
    )
    grad_query_bf = grad_query_raw.reshape(row_count, HEADS * HDIM).astype(jnp.bfloat16)
    grad_key_bf = grad_key_raw[:, 0, :].astype(jnp.bfloat16)
    grad_value_bf = grad_value.astype(jnp.bfloat16)
    grad_w_query = dot_f32(attn_in.T, grad_query_bf)
    grad_w_key = dot_f32(attn_in.T, grad_key_bf)
    grad_w_value = dot_f32(attn_in.T, grad_value_bf)
    grad_attn_in = (
        dot_f32(grad_query_bf, query_w.T)
        + dot_f32(grad_key_bf, key_w.T)
        + dot_f32(grad_value_bf, value_w.T)
    )
    grad_in_part, grad_gain_one = rms_backward(resid_in, factor_one, gain_one, grad_attn_in)
    input_grad = grad_mid + grad_in_part
    (
        half_query,
        half_key,
        half_value,
        half_out,
        half_gate,
        half_up,
        half_down,
        half_one,
        half_qgain,
        half_kgain,
        half_two,
        half_three,
        half_four,
    ) = (
        lax.psum_scatter(
            grad_w_query.astype(jnp.bfloat16), "wsh", scatter_dimension=1, tiled=True
        ).astype(jnp.float32),
        lax.psum_scatter(
            grad_w_key.astype(jnp.bfloat16), "wsh", scatter_dimension=1, tiled=True
        ).astype(jnp.float32),
        lax.psum_scatter(
            grad_w_value.astype(jnp.bfloat16), "wsh", scatter_dimension=1, tiled=True
        ).astype(jnp.float32),
        lax.psum_scatter(
            grad_w_out.astype(jnp.bfloat16), "wsh", scatter_dimension=0, tiled=True
        ).astype(jnp.float32),
        lax.psum_scatter(
            grad_w_gate.astype(jnp.bfloat16), "wsh", scatter_dimension=1, tiled=True
        ).astype(jnp.float32),
        lax.psum_scatter(
            grad_w_up.astype(jnp.bfloat16), "wsh", scatter_dimension=1, tiled=True
        ).astype(jnp.float32),
        lax.psum_scatter(
            grad_w_down.astype(jnp.bfloat16), "wsh", scatter_dimension=0, tiled=True
        ).astype(jnp.float32),
        lax.psum_scatter(
            grad_gain_one.astype(jnp.bfloat16), "wsh", scatter_dimension=0, tiled=True
        ).astype(jnp.float32),
        lax.psum_scatter(
            grad_gain_query.astype(jnp.bfloat16), "wsh", scatter_dimension=0, tiled=True
        ).astype(jnp.float32),
        lax.psum_scatter(
            grad_gain_key.astype(jnp.bfloat16), "wsh", scatter_dimension=0, tiled=True
        ).astype(jnp.float32),
        lax.psum_scatter(
            grad_gain_two.astype(jnp.bfloat16), "wsh", scatter_dimension=0, tiled=True
        ).astype(jnp.float32),
        lax.psum_scatter(
            grad_gain_three.astype(jnp.bfloat16), "wsh", scatter_dimension=0, tiled=True
        ).astype(jnp.float32),
        lax.psum_scatter(
            grad_gain_four.astype(jnp.bfloat16), "wsh", scatter_dimension=0, tiled=True
        ).astype(jnp.float32),
    )
    (
        sum_query,
        sum_key,
        sum_value,
        sum_out,
        sum_gate,
        sum_up,
        sum_down,
        sum_one,
        sum_qgain,
        sum_kgain,
        sum_two,
        sum_three,
        sum_four,
    ) = lax.psum(
        (
            half_query,
            half_key,
            half_value,
            half_out,
            half_gate,
            half_up,
            half_down,
            half_one,
            half_qgain,
            half_kgain,
            half_two,
            half_three,
            half_four,
        ),
        "ctx",
    )
    return (
        block_output[None],
        input_grad[None],
        sum_query,
        sum_key,
        sum_value,
        sum_out,
        sum_gate,
        sum_up,
        sum_down,
        sum_one,
        sum_qgain,
        sum_kgain,
        sum_two,
        sum_three,
        sum_four,
    )


def solution(mesh):
    return jax.shard_map(
        per_device,
        mesh=mesh,
        in_specs=(
            P("wsh", "ctx", None),
            P("wsh", "ctx", None),
            P(),
            P(None, "wsh"),
            P(None, "wsh"),
            P(None, "wsh"),
            P("wsh", None),
            P(None, "wsh"),
            P(None, "wsh"),
            P("wsh", None),
            P("wsh"),
            P("wsh"),
            P("wsh"),
            P("wsh"),
            P("wsh"),
            P("wsh"),
        ),
        out_specs=(
            P("wsh", "ctx", None),
            P("wsh", "ctx", None),
            P(None, "wsh"),
            P(None, "wsh"),
            P(None, "wsh"),
            P("wsh", None),
            P(None, "wsh"),
            P(None, "wsh"),
            P("wsh", None),
            P("wsh"),
            P("wsh"),
            P("wsh"),
            P("wsh"),
            P("wsh"),
            P("wsh"),
        ),
        check_vma=False,
    )
```

profile of v0, /device:TPU:0, one launch (start us, length us, event | category | flops | bytes accessed | tf_op | source)
XLA Modules:
  0.0 1200.0 jit_solution(14206055669539594924)
XLA Ops:
  35.8 4.4 broadcast_compare_fusion
  43.0 55.2 %all-gather.23.cloned.1.call-done = bf16[8192,1,256]{2,0,1:T(8,128)(2,1)} async-done(((bf16[128,1,256]{2,0,1:T(8,128)(2,1)}), bf16[8192,1,256]{2,0,1:T(8,128)(2,1)}) %all-gather.23.cloned.1.call-update) | async-done | bytes 4194320 | tf_op jit(solution)/shard_map/all_gather | solution.py:144
  98.1 10.4 fusion.81
  108.6 8.0 fusion.2
  116.6 51.4 %all-gather.11.cloned.1.call-done = bf16[8192,256]{1,0:T(8,128)(2,1)} async-done(((bf16[128,256]{1,0:T(8,128)(2,1)}), bf16[8192,256]{1,0:T(8,128)(2,1)}) %all-gather.11.cloned.1.call-update) | async-done | bytes 4194320 | tf_op jit(solution)/shard_map/all_gather | solution.py:145
  168.1 9.7 fusion.19
  181.3 14.8 %all-gather.17.cloned.1.call-done = bf16[640,2048]{1,0:T(8,128)(2,1)} async-done(((bf16[640,1024]{1,0:T(8,128)(2,1)}), bf16[640,2048]{1,0:T(8,128)(2,1)}) %all-gather.17.cloned.1.call-update) | async-done | bytes 2621456 | tf_op jit(solution)/shard_map/all_gather | solution.py:120
  198.4 14.7 %all-gather.19.cloned.1.call-done = bf16[640,2048]{1,0:T(8,128)(2,1)} async-done(((bf16[640,1024]{1,0:T(8,128)(2,1)}), bf16[640,2048]{1,0:T(8,128)(2,1)}) %all-gather.19.cloned.1.call-update) | async-done | bytes 2621456 | tf_op jit(solution)/shard_map/all_gather | solution.py:121
  213.0 3.5 multiply_convert_fusion.1
  216.5 13.6 %all-gather.21.cloned.1.call-done = bf16[2048,640]{1,0:T(8,128)(2,1)} async-done(((bf16[1024,640]{1,0:T(8,128)(2,1)}), bf16[2048,640]{1,0:T(8,128)(2,1)}) %all-gather.21.cloned.1.call-update) | async-done | bytes 2621456 | tf_op jit(solution)/shard_map/all_gather | solution.py:122
  241.6 11.6 convolution_bitcast_fusion
  253.2 8.8 fusion.1
  262.0 3.8 fusion.4
  268.6 6.3 pad_maximum_fusion
  274.9 8.0 fusion.16
  296.5 367.4 %reduce-scatter.13.cloned.1.call-done = f32[128,512]{1,0:T(8,128)} async-done(((f32[8192,512]{1,0:T(8,128)}), f32[128,512]{1,0:T(8,128)}) %reduce-scatter.13.cloned.1.call-update) | async-done | bytes 262160 | tf_op jit(solution)/shard_map/reduce_scatter | solution.py:207
  667.4 6.5 reduce-scatter.15.cloned.1.call-done
  674.0 15.7 %reduce-scatter.17.cloned.1.call-done = bf16[512,640]{1,0:T(8,128)(2,1)} async-done(((bf16[1024,640]{1,0:T(8,128)(2,1)}), bf16[512,640]{1,0:T(8,128)(2,1)}) %reduce-scatter.17.cloned.1.call-update) | async-done | bytes 655376 | tf_op jit(solution)/shard_map/reduce_scatter | solution.py:253
  689.7 17.2 %reduce-scatter.19.cloned.1.call-done = bf16[640,1024]{1,0:T(8,128)(2,1)} async-done(((bf16[640,2048]{1,0:T(8,128)(2,1)}), bf16[640,1024]{1,0:T(8,128)(2,1)}) %reduce-scatter.19.cloned.1.call-update) | async-done | bytes 1310736 | tf_op jit(solution)/shard_map/reduce_scatter | solution.py:256
  707.0 17.2 %reduce-scatter.21.cloned.1.call-done = bf16[640,1024]{1,0:T(8,128)(2,1)} async-done(((bf16[640,2048]{1,0:T(8,128)(2,1)}), bf16[640,1024]{1,0:T(8,128)(2,1)}) %reduce-scatter.21.cloned.1.call-update) | async-done | bytes 1310736 | tf_op jit(solution)/shard_map/reduce_scatter | solution.py:259
  724.2 17.2 %reduce-scatter.23.cloned.1.call-done = bf16[1024,640]{1,0:T(8,128)(2,1)} async-done(((bf16[2048,640]{1,0:T(8,128)(2,1)}), bf16[1024,640]{1,0:T(8,128)(2,1)}) %reduce-scatter.23.cloned.1.call-update) | async-done | bytes 1310736 | tf_op jit(solution)/shard_map/reduce_scatter | solution.py:262
  749.8 5.8 reduce-scatter.25.cloned.1.call-done
  756.6 13.5 %reduce-scatter.27.cloned.1.call-done = bf16[128,640]{1,0:T(8,128)(2,1)} async-done(((bf16[256,640]{1,0:T(8,128)(2,1)}), bf16[128,640]{1,0:T(8,128)(2,1)}) %reduce-scatter.27.cloned.1.call-update) | async-done | bytes 163856
  771.2 422.1 %all-reduce.14 = (f32[640,512]{1,0:T(8,128)}, f32[640,128]{1,0:T(8,128)}, f32[640,128]{1,0:T(8,128)}, f32[512,640]{1,0:T(8,128)}, f32[640,1024]{1,0:T(8,128)}, /...) all-reduce(bf16[640,512]{1,0:T(8,128)(2,1)} %reduce-scatter.15.clon, ...), channel_id=1, replica_groups=mesh['ctx'=64,'wsh'=2] {'ctx'}, use_global_device_ids=true, to_apply=%region_17.18 | all-reduce | flops 2786816 | bytes 16723968 | tf_op jit(solution)/shard_map/psum | solution.py:298
  (226 shorter events, 76.2 us)
Async XLA Ops:
  7.2 33.1 %all-gather.13.cloned.1.call-start = ((), (), s32[]{:S(2)}) async-start(), calls=%async_computation.9 | async-start | bytes 1966080 | tf_op jit(solution)/shard_map/all_gather | solution.py:116
  7.9 90.2 %all-gather.23.cloned.1.call-start = ((), (), s32[]{:S(2)}) async-start(), calls=%async_computation.20 | async-start | bytes 4259840 | tf_op jit(solution)/shard_map/all_gather | solution.py:144
  25.9 142.2 %all-gather.11.cloned.1.call-start = ((), (), s32[]{:S(2)}) async-start(), calls=%async_computation.8 | async-start | bytes 4259840 | tf_op jit(solution)/shard_map/all_gather | solution.py:145
  30.7 148.4 %all-gather.15.cloned.1.call-start = ((), (), s32[]{:S(2)}) async-start(), calls=%async_computation.10 | async-start | bytes 1966080 | tf_op jit(solution)/shard_map/all_gather | solution.py:119
  31.3 164.7 %all-gather.17.cloned.1.call-start = ((), (), s32[]{:S(2)}) async-start(), calls=%async_computation.11 | async-start | bytes 3932160 | tf_op jit(solution)/shard_map/all_gather | solution.py:120
  31.9 181.1 %all-gather.19.cloned.1.call-start = ((), (), s32[]{:S(2)}) async-start(), calls=%async_computation.12 | async-start | bytes 3932160 | tf_op jit(solution)/shard_map/all_gather | solution.py:121
  32.5 197.6 %all-gather.21.cloned.1.call-start = ((), (), s32[]{:S(2)}) async-start(), calls=%async_computation.13 | async-start | bytes 3932160 | tf_op jit(solution)/shard_map/all_gather | solution.py:122
  33.2 630.6 %reduce-scatter.13.cloned.1.call-start = ((), (), s32[]{:S(2)}) async-start(), calls=%async_computation.14 | async-start | bytes 17039360 | tf_op jit(solution)/shard_map/reduce_scatter | solution.py:207
  274.9 399.1 %reduce-scatter.15.cloned.1.call-start = ((), (), s32[]{:S(2)}) async-start(), calls=%async_computation.15 | async-start | bytes 1966080 | tf_op jit(solution)/shard_map/reduce_scatter | solution.py:244
  285.9 403.9 %reduce-scatter.17.cloned.1.call-start = ((), (), s32[]{:S(2)}) async-start(), calls=%async_computation.16 | async-start | bytes 1966080 | tf_op jit(solution)/shard_map/reduce_scatter | solution.py:253
  287.5 419.5 %reduce-scatter.19.cloned.1.call-start = ((), (), s32[]{:S(2)}) async-start(), calls=%async_computation.17 | async-start | bytes 3932160 | tf_op jit(solution)/shard_map/reduce_scatter | solution.py:256
  290.0 434.2 %reduce-scatter.21.cloned.1.call-start = ((), (), s32[]{:S(2)}) async-start(), calls=%async_computation.18 | async-start | bytes 3932160 | tf_op jit(solution)/shard_map/reduce_scatter | solution.py:259
  292.6 372.3 %copy-start.41 = (f32[128]{0:T(128)S(1)}, f32[128]{0:T(128)}, u32[]{:S(2)}) copy-start(f32[128]{0:T(128)} %copy-done.40) | copy-start | bytes 1540
  292.6 372.3 %copy-start.45 = (f32[128]{0:T(128)S(1)}, f32[128]{0:T(128)}, u32[]{:S(2)}) copy-start(f32[128]{0:T(128)} %copy-done.44) | copy-start | bytes 1540
  292.6 372.7 %copy-start.28 = (f32[128,256]{1,0:T(8,128)S(1)}, f32[128,256]{1,0:T(8,128)}, u32[]{:S(2)}) copy-start(f32[128,256]{1,0:T(8,128)} %copy-done.27) | copy-start | bytes 393220
  292.6 372.7 %copy-start.43 = (f32[128]{0:T(128)S(1)}, f32[128]{0:T(128)}, u32[]{:S(2)}) copy-start(f32[128]{0:T(128)} %copy-done.42) | copy-start | bytes 1540
  292.6 374.3 %copy-start.5 = (bf16[640,1024]{1,0:T(8,128)(2,1)S(1)}, bf16[640,1024]{1,0:T(8,128)(2,1)}, u32[]{:S(2)}) copy-start(bf16[640,1024]{1,0:T(8,128)(2,1)} %all-gather.13.cloned.1.call-done) | copy-start | bytes 3932164
  292.6 448.8 %reduce-scatter.23.cloned.1.call-start = ((), (), s32[]{:S(2)}) async-start(), calls=%async_computation.19 | async-start | bytes 3932160 | tf_op jit(solution)/shard_map/reduce_scatter | solution.py:262
  295.1 447.6 %copy-start.23 = (bf16[640,256]{1,0:T(8,128)(2,1)S(1)}, bf16[640,256]{1,0:T(8,128)(2,1)}, u32[]{:S(2)}) copy-start(bf16[640,256]{1,0:T(8,128)(2,1)} %copy-done.22) | copy-start | bytes 983044
  295.1 460.4 %reduce-scatter.25.cloned.1.call-start = ((), (), s32[]{:S(2)}) async-start(), calls=%async_computation.21 | async-start | bytes 491520
  664.9 80.2 %copy-start.39 = (bf16[640]{0:T(1024)(128)(2,1)S(1)}, bf16[640]{0:T(1024)(128)(2,1)}, u32[]{:S(2)}) copy-start(bf16[640]{0:T(1024)(128)(2,1)} %get-tuple-element.17) | copy-start | bytes 3844
  664.9 80.2 %copy-start.47 = (bf16[256]{0:T(256)(128)(2,1)S(1)}, bf16[256]{0:T(256)(128)(2,1)}, u32[]{:S(2)}) copy-start(bf16[256]{0:T(256)(128)(2,1)} %get-tuple-element.15) | copy-start | bytes 1540
  664.9 83.0 %copy-start.11 = (f32[128,640]{1,0:T(8,128)S(1)}, f32[128,640]{1,0:T(8,128)}, u32[]{:S(2)}) copy-start(f32[128,640]{1,0:T(8,128)} %copy-done.10) | copy-start | bytes 983044
  666.8 103.2 %reduce-scatter.27.cloned.1.call-start = ((), (), s32[]{:S(2)}) async-start(), calls=%async_computation.22 | async-start | bytes 491520
  (40 other events, 732.9 us)
Sparse Core Ops, SparseCore 0:
  9.7 14.5 all-gather.12
  27.7 70.3 all-gather.22
  101.6 66.4 all-gather.10
  169.6 9.5 all-gather.14
  180.6 15.3 all-gather.16
  197.6 15.4 all-gather.18
  214.7 15.3 all-gather.20
  275.0 388.8 reduce-scatter.12
  666.8 7.1 reduce-scatter.14
  676.9 12.8 reduce-scatter.16
  692.7 14.2 reduce-scatter.18
  709.9 14.2 reduce-scatter.20
  727.1 14.2 reduce-scatter.22
  743.7 11.7 reduce-scatter.24
  758.3 11.7 reduce-scatter.26
where the time goes:
time: 1210 us; the launch traced here: 1200 us
  waiting for transfers between devices  615 us (51%)
  blocking collectives  435 us (36%)
  matrix products  84 us (7%)
  other arithmetic  30.5 us (3%)
  local copies, waits for them, and re-layouts  17.7 us (1%)
  between operations  17 us (1%)
    psum x1, blocking collectives, per_device(): lax.psum((half_query, half_key, half_value, half_out, half_gate, half_up,...  422 us
    reduce_scatter x1, waiting for transfers between devices, per_device(): kv_mine = lax.psum_scatter(kv_terms, 'ctx', scatter_dimension=0, tiled=True)  367 us
    all_gather x1, waiting for transfers between devices, per_device(): lax.all_gather(key_rot, 'ctx', axis=0, tiled=True)  55.2 us
    all_gather x1, waiting for transfers between devices, per_device(): lax.all_gather(value_bf, 'ctx', axis=0, tiled=True)  51.4 us
    dot_general x21, matrix products, dot_f32(): return jnp.dot(left, right, preferred_element_type=jnp.float32)  31.7 us
  transfers between devices with their start and end apart: 15, of which 14 were waited for; matrix products, arithmetic and copies ran while one was open for 7% of the time, Pallas kernels for 0%

commit v1 on v0

--- a/solution.py
+++ b/solution.py
@@ -141,7 +141,9 @@
     query_rot = rotate(query_normed, cos_tab, sin_tab).astype(jnp.bfloat16)
     key_rot = rotate(key_normed, cos_tab, sin_tab)[:, 0, :].astype(jnp.bfloat16)
     key_all, value_all = (
-        lax.all_gather(key_rot, "ctx", axis=0, tiled=True),
+        jnp.concatenate(
+            lax.all_to_all(jnp.stack([key_rot] * lax.axis_size("ctx")), "ctx", 0, 0), axis=0
+        ),
         lax.all_gather(value_bf, "ctx", axis=0, tiled=True),
     )
     scores = masked_scores(query_rot, key_all, query_pos, key_pos)

time: 1210 us -> 1180 us (0.975)
  waiting for transfers between devices: 615 us -> 572 us
    all_gather x1 -> x0, waiting for transfers between devices: 55.2 us -> none  [per_device(): lax.all_gather(key_rot, 'ctx', axis=0, tiled=True)]
    all_to_all x0 -> x1, waiting for transfers between devices: none -> 44.9 us  [per_device(): lax.all_to_all(jnp.stack([key_rot] * lax.axis_size('ctx')), 'ctx', 0, 0)]
    all_gather x1, waiting for transfers between devices: 51.4 us -> 20.1 us  [per_device(): lax.all_gather(value_bf, 'ctx', axis=0, tiled=True)]
where the time goes in v1:
time: 1180 us; the launch traced here: 1170 us
  waiting for transfers between devices  572 us (48%)
  blocking collectives  435 us (37%)
  matrix products  83.1 us (7%)
  other arithmetic  29.3 us (2%)
  local copies, waits for them, and re-layouts  19.5 us (2%)
  between operations  17 us (1%)
  starting transfers between devices  12.7 us (1%)
    psum x1, blocking collectives, per_device(): lax.psum((half_query, half_key, half_value, half_out, half_gate, half_up,...  422 us
    reduce_scatter x1, waiting for transfers between devices, per_device(): kv_mine = lax.psum_scatter(kv_terms, 'ctx', scatter_dimension=0, tiled=True)  368 us
    all_to_all x1, waiting for transfers between devices, per_device(): lax.all_to_all(jnp.stack([key_rot] * lax.axis_size('ctx')), 'ctx', 0, 0)  44.9 us
    dot_general x21, matrix products, dot_f32(): return jnp.dot(left, right, preferred_element_type=jnp.float32)  30.8 us
  transfers between devices with their start and end apart: 15, of which 14 were waited for; matrix products, arithmetic and copies ran while one was open for 7% of the time, Pallas kernels for 0%

profile of v1, /device:TPU:0, one launch (start us, length us, event | category | flops | bytes accessed | tf_op | source)
XLA Modules:
  0.0 1168.7 jit_solution(2612246335440572044)
XLA Ops:
  31.9 11.9 %all-to-all-start = ((bf16[64,128,256]{2,1,0:T(8,128)(2,1)}), bf16[64,128,256]{2,1,0:T(8,128)(2,1)}, u32[]{:S(2)}, u32[]{:S(2)}) async-start(bf16[64,128,256]{2,1,0:T(8,128)(2,1)} %stack.2), calls=%async_computation | async-start | bytes 8388608 | tf_op jit(solution)/shard_map/all_to_all | solution.py:145
  47.0 4.5 broadcast_compare_fusion
  54.1 44.9 %all-to-all-done = bf16[64,128,256]{2,1,0:T(8,128)(2,1)} async-done(((bf16[64,128,256]{2,1,0:T(8,128)(2,1)}), bf16[64,128,256]{2,1,0:T(8,128)(2,1)}, u32[]{:S(2)}, u32[]{:S(2)}) %all-to-all-start) | async-done | bytes 4194336 | tf_op jit(solution)/shard_map/all_to_all | solution.py:145
  99.0 10.5 fusion.73
  109.5 8.0 fusion.2
  117.5 20.1 %all-gather.9.cloned.1.call-done = bf16[8192,256]{1,0:T(8,128)(2,1)} async-done(((bf16[128,256]{1,0:T(8,128)(2,1)}), bf16[8192,256]{1,0:T(8,128)(2,1)}) %all-gather.9.cloned.1.call-update) | async-done | bytes 4194320 | tf_op jit(solution)/shard_map/all_gather | solution.py:147
  137.6 9.7 fusion.11
  150.9 14.8 %all-gather.15.cloned.1.call-done = bf16[640,2048]{1,0:T(8,128)(2,1)} async-done(((bf16[640,1024]{1,0:T(8,128)(2,1)}), bf16[640,2048]{1,0:T(8,128)(2,1)}) %all-gather.15.cloned.1.call-update) | async-done | bytes 2621456 | tf_op jit(solution)/shard_map/all_gather | solution.py:120
  168.0 14.7 %all-gather.17.cloned.1.call-done = bf16[640,2048]{1,0:T(8,128)(2,1)} async-done(((bf16[640,1024]{1,0:T(8,128)(2,1)}), bf16[640,2048]{1,0:T(8,128)(2,1)}) %all-gather.17.cloned.1.call-update) | async-done | bytes 2621456 | tf_op jit(solution)/shard_map/all_gather | solution.py:121
  186.2 13.4 %all-gather.19.cloned.1.call-done = bf16[2048,640]{1,0:T(8,128)(2,1)} async-done(((bf16[1024,640]{1,0:T(8,128)(2,1)}), bf16[2048,640]{1,0:T(8,128)(2,1)}) %all-gather.19.cloned.1.call-update) | async-done | bytes 2621456 | tf_op jit(solution)/shard_map/all_gather | solution.py:122
  211.1 11.6 convolution_bitcast_fusion
  222.7 8.8 fusion.1
  231.5 3.8 fusion.4
  238.1 6.3 pad_maximum_fusion
  244.4 8.0 fusion.10
  266.0 367.7 %reduce-scatter.13.cloned.1.call-done = f32[128,512]{1,0:T(8,128)} async-done(((f32[8192,512]{1,0:T(8,128)}), f32[128,512]{1,0:T(8,128)}) %reduce-scatter.13.cloned.1.call-update) | async-done | bytes 262160 | tf_op jit(solution)/shard_map/reduce_scatter | solution.py:209
  637.2 5.5 reduce-scatter.15.cloned.1.call-done
  642.7 15.9 %reduce-scatter.17.cloned.1.call-done = bf16[512,640]{1,0:T(8,128)(2,1)} async-done(((bf16[1024,640]{1,0:T(8,128)(2,1)}), bf16[512,640]{1,0:T(8,128)(2,1)}) %reduce-scatter.17.cloned.1.call-update) | async-done | bytes 655376 | tf_op jit(solution)/shard_map/reduce_scatter | solution.py:255
  658.6 17.1 %reduce-scatter.19.cloned.1.call-done = bf16[640,1024]{1,0:T(8,128)(2,1)} async-done(((bf16[640,2048]{1,0:T(8,128)(2,1)}), bf16[640,1024]{1,0:T(8,128)(2,1)}) %reduce-scatter.19.cloned.1.call-update) | async-done | bytes 1310736 | tf_op jit(solution)/shard_map/reduce_scatter | solution.py:258
  675.7 17.4 %reduce-scatter.21.cloned.1.call-done = bf16[640,1024]{1,0:T(8,128)(2,1)} async-done(((bf16[640,2048]{1,0:T(8,128)(2,1)}), bf16[640,1024]{1,0:T(8,128)(2,1)}) %reduce-scatter.21.cloned.1.call-update) | async-done | bytes 1310736 | tf_op jit(solution)/shard_map/reduce_scatter | solution.py:261
  693.1 17.1 %reduce-scatter.23.cloned.1.call-done = bf16[1024,640]{1,0:T(8,128)(2,1)} async-done(((bf16[2048,640]{1,0:T(8,128)(2,1)}), bf16[1024,640]{1,0:T(8,128)(2,1)}) %reduce-scatter.23.cloned.1.call-update) | async-done | bytes 1310736 | tf_op jit(solution)/shard_map/reduce_scatter | solution.py:264
  718.5 5.9 reduce-scatter.25.cloned.1.call-done
  725.5 13.5 %reduce-scatter.27.cloned.1.call-done = bf16[128,640]{1,0:T(8,128)(2,1)} async-done(((bf16[256,640]{1,0:T(8,128)(2,1)}), bf16[128,640]{1,0:T(8,128)(2,1)}) %reduce-scatter.27.cloned.1.call-update) | async-done | bytes 163856
  740.1 421.9 %all-reduce.14 = (f32[640,512]{1,0:T(8,128)}, f32[640,128]{1,0:T(8,128)}, f32[640,128]{1,0:T(8,128)}, f32[512,640]{1,0:T(8,128)}, f32[640,1024]{1,0:T(8,128)}, /...) all-reduce(bf16[640,512]{1,0:T(8,128)(2,1)} %reduce-scatter.15.clon, ...), channel_id=1, replica_groups=mesh['ctx'=64,'wsh'=2] {'ctx'}, use_global_device_ids=true, to_apply=%region_17.18 | all-reduce | flops 2786816 | bytes 16723968 | tf_op jit(solution)/shard_map/psum | solution.py:300
  (230 shorter events, 79.0 us)
Async XLA Ops:
  7.2 44.2 %all-gather.11.cloned.1.call-start = ((), (), s32[]{:S(2)}) async-start(), calls=%async_computation.10 | async-start | bytes 1966080 | tf_op jit(solution)/shard_map/all_gather | solution.py:116
  8.0 129.6 %all-gather.9.cloned.1.call-start = ((), (), s32[]{:S(2)}) async-start(), calls=%async_computation.9 | async-start | bytes 4259840 | tf_op jit(solution)/shard_map/all_gather | solution.py:147
  21.2 127.6 %all-gather.13.cloned.1.call-start = ((), (), s32[]{:S(2)}) async-start(), calls=%async_computation.11 | async-start | bytes 1966080 | tf_op jit(solution)/shard_map/all_gather | solution.py:119
  21.9 143.8 %all-gather.15.cloned.1.call-start = ((), (), s32[]{:S(2)}) async-start(), calls=%async_computation.12 | async-start | bytes 3932160 | tf_op jit(solution)/shard_map/all_gather | solution.py:120
  22.5 160.2 %all-gather.17.cloned.1.call-start = ((), (), s32[]{:S(2)}) async-start(), calls=%async_computation.13 | async-start | bytes 3932160 | tf_op jit(solution)/shard_map/all_gather | solution.py:121
  31.9 67.1 %all-to-all-start = ((bf16[64,128,256]{2,1,0:T(8,128)(2,1)}), bf16[64,128,256]{2,1,0:T(8,128)(2,1)}, u32[]{:S(2)}, u32[]{:S(2)}) async-start(bf16[64,128,256]{2,1,0:T(8,128)(2,1)} %stack.2), calls=%async_computation | async-start | bytes 8388608 | tf_op jit(solution)/shard_map/all_to_all | solution.py:145
  43.8 155.8 %all-gather.19.cloned.1.call-start = ((), (), s32[]{:S(2)}) async-start(), calls=%async_computation.14 | async-start | bytes 3932160 | tf_op jit(solution)/shard_map/all_gather | solution.py:122
  44.4 589.3 %reduce-scatter.13.cloned.1.call-start = ((), (), s32[]{:S(2)}) async-start(), calls=%async_computation.15 | async-start | bytes 17039360 | tf_op jit(solution)/shard_map/reduce_scatter | solution.py:209
  244.4 398.3 %reduce-scatter.15.cloned.1.call-start = ((), (), s32[]{:S(2)}) async-start(), calls=%async_computation.16 | async-start | bytes 1966080 | tf_op jit(solution)/shard_map/reduce_scatter | solution.py:246
  255.4 403.2 %reduce-scatter.17.cloned.1.call-start = ((), (), s32[]{:S(2)}) async-start(), calls=%async_computation.17 | async-start | bytes 1966080 | tf_op jit(solution)/shard_map/reduce_scatter | solution.py:255
  257.0 418.7 %reduce-scatter.19.cloned.1.call-start = ((), (), s32[]{:S(2)}) async-start(), calls=%async_computation.18 | async-start | bytes 3932160 | tf_op jit(solution)/shard_map/reduce_scatter | solution.py:258
  259.5 433.6 %reduce-scatter.21.cloned.1.call-start = ((), (), s32[]{:S(2)}) async-start(), calls=%async_computation.19 | async-start | bytes 3932160 | tf_op jit(solution)/shard_map/reduce_scatter | solution.py:261
  262.1 372.5 %copy-start.44 = (f32[128]{0:T(128)S(1)}, f32[128]{0:T(128)}, u32[]{:S(2)}) copy-start(f32[128]{0:T(128)} %copy-done.43) | copy-start | bytes 1540
  262.1 372.5 %copy-start.46 = (f32[128]{0:T(128)S(1)}, f32[128]{0:T(128)}, u32[]{:S(2)}) copy-start(f32[128]{0:T(128)} %copy-done.45) | copy-start | bytes 1540
  262.1 372.9 %copy-start.28 = (f32[128,256]{1,0:T(8,128)S(1)}, f32[128,256]{1,0:T(8,128)}, u32[]{:S(2)}) copy-start(f32[128,256]{1,0:T(8,128)} %copy-done.27) | copy-start | bytes 393220
  262.1 372.9 %copy-start.42 = (f32[128]{0:T(128)S(1)}, f32[128]{0:T(128)}, u32[]{:S(2)}) copy-start(f32[128]{0:T(128)} %copy-done.41) | copy-start | bytes 1540
  262.1 374.5 %copy-start.5 = (bf16[640,1024]{1,0:T(8,128)(2,1)S(1)}, bf16[640,1024]{1,0:T(8,128)(2,1)}, u32[]{:S(2)}) copy-start(bf16[640,1024]{1,0:T(8,128)(2,1)} %all-gather.11.cloned.1.call-done) | copy-start | bytes 3932164
  262.2 448.0 %reduce-scatter.23.cloned.1.call-start = ((), (), s32[]{:S(2)}) async-start(), calls=%async_computation.20 | async-start | bytes 3932160 | tf_op jit(solution)/shard_map/reduce_scatter | solution.py:264
  264.6 446.8 %copy-start.23 = (bf16[640,256]{1,0:T(8,128)(2,1)S(1)}, bf16[640,256]{1,0:T(8,128)(2,1)}, u32[]{:S(2)}) copy-start(bf16[640,256]{1,0:T(8,128)(2,1)} %copy-done.22) | copy-start | bytes 983044
  264.6 459.8 %reduce-scatter.25.cloned.1.call-start = ((), (), s32[]{:S(2)}) async-start(), calls=%async_computation.21 | async-start | bytes 491520
  634.7 79.2 %copy-start.40 = (bf16[640]{0:T(1024)(128)(2,1)S(1)}, bf16[640]{0:T(1024)(128)(2,1)}, u32[]{:S(2)}) copy-start(bf16[640]{0:T(1024)(128)(2,1)} %get-tuple-element.17) | copy-start | bytes 3844
  634.7 79.2 %copy-start.48 = (bf16[256]{0:T(256)(128)(2,1)S(1)}, bf16[256]{0:T(256)(128)(2,1)}, u32[]{:S(2)}) copy-start(bf16[256]{0:T(256)(128)(2,1)} %get-tuple-element.15) | copy-start | bytes 1540
  634.7 82.0 %copy-start.11 = (f32[128,640]{1,0:T(8,128)S(1)}, f32[128,640]{1,0:T(8,128)}, u32[]{:S(2)}) copy-start(f32[128,640]{1,0:T(8,128)} %copy-done.10) | copy-start | bytes 983044
  636.6 102.4 %reduce-scatter.27.cloned.1.call-start = ((), (), s32[]{:S(2)}) async-start(), calls=%async_computation.22 | async-start | bytes 491520
  (42 other events, 680.1 us)
Sparse Core Ops, SparseCore 0:
  9.7 14.5 all-gather.10
  27.7 109.7 all-gather.8
  139.2 9.5 all-gather.12
  150.3 15.3 all-gather.14
  167.2 15.4 all-gather.16
  184.2 15.3 all-gather.18
  244.5 389.1 reduce-scatter.12
  636.6 6.0 reduce-scatter.14
  645.8 12.8 reduce-scatter.16
  661.4 14.2 reduce-scatter.18
  678.7 14.2 reduce-scatter.20
  695.9 14.2 reduce-scatter.22
  712.6 11.7 reduce-scatter.24
  727.2 11.7 reduce-scatter.26
